TPU v7x, 32 devices: a whole 2x2x4 slice. The times are simulated.
32 devices in a mesh: occ: 8 (over y, x, core), ao: 4 (over z).
Axes of the slice: x: 2, y: 2, z: 4, core: 2. Of those that a mesh axis runs over, the one named last changes fastest.
Arguments:
- coef: bfloat16 [2048, 8], P('ao', 'occ'), may hold values from -0.5 to 0.5
- half_ints: bfloat16 [8, 1024, 2048], P('occ', None, 'ao'), may hold values from -0.5 to 0.5
- metric_inv: bfloat16 [64, 128, 128], replicated, may hold values from -1 to 2, as said below
- dom_blocks: int32 [8, 8], P('occ'), may hold values from 0 to 63, as said below
- dom_len: int32 [8], P('occ'), may hold values from 2 to 8
Outputs:
- exchange_k: float32 [2048, 2048], P('ao', 'occ')
- fit_density: float32 [8192], replicated
Inputs may be any that keep to these rules, and one draw needn't show every extreme that they name: `dom_blocks`: each row holds 8 different block numbers. `metric_inv`: full rank blocks.
All inputs are finite; a program needn't handle non-finite values.
Results may differ from a plain program's by a relative error of at most 0.0055.
Values may be sent and summed in bfloat16 or wider, within the bound.
No kernel may reach another device: no remote copies, remote signals or barrier semaphores. Data moves between devices by JAX's collectives and lax.ppermute only.
A program may use at most 128 MiB of HBM per device.

v0:
```python
import jax
import jax.numpy as jnp
from jax import lax
from jax.sharding import PartitionSpec as P


def on_device(coef, half_ints, metric_inv, dom_blocks, dom_len):
    lmo_count, domain, ao_rows = half_ints.shape
    block = metric_inv.shape[1]
    slots = domain // block
    fit_blocks = metric_inv.shape[0]
    metric_rows = metric_inv[dom_blocks]
    raw_ints = half_ints.reshape(lmo_count, slots, block, ao_rows)
    fitted = jnp.einsum(
        "isab,isbm->isam", metric_rows, raw_ints, preferred_element_type=jnp.float32
    )
    live_slots = jnp.arange(slots, dtype=jnp.int32)[None, :] < dom_len[:, None]
    fitted = jnp.where(live_slots[:, :, None, None], fitted, 0.0)
    fitted = fitted.reshape(lmo_count, domain, ao_rows).astype(jnp.bfloat16)
    pair_part = jnp.einsum("ipm,mi->ip", fitted, coef, preferred_element_type=jnp.float32)
    one_hot = (
        dom_blocks[:, :, None] == jnp.arange(fit_blocks, dtype=jnp.int32)[None, None, :]
    ).astype(jnp.float32)
    local_density = jnp.einsum("isf,isr->fr", one_hot, pair_part.reshape(lmo_count, slots, block))
    density = lax.psum(local_density, ("occ", "ao"))
    density = density.reshape(fit_blocks * block)
    partial_value = jnp.einsum(
        "ipm,ipn->mn",
        fitted,
        lax.all_gather(fitted, "ao", axis=2, tiled=True),
        preferred_element_type=jnp.float32,
    )
    exchange_k = lax.psum_scatter(partial_value, "occ", scatter_dimension=1, tiled=True)
    return (exchange_k, density)


def solution(mesh):
    in_specs = (P("ao", "occ"), P("occ", None, "ao"), P(), P("occ", None), P("occ"))
    out_specs = (P("ao", "occ"), P())
    return jax.shard_map(
        on_device, mesh=mesh, in_specs=in_specs, out_specs=out_specs, check_vma=False
    )
```

profile of v0, /device:TPU:0, one launch (start us, length us, event | category | flops | bytes accessed | tf_op | source)
XLA Modules:
  0.0 159.3 jit_solution(12443113816982479165)
XLA Ops:
  7.2 0.0 copy-start
  7.2 0.0 all-gather.2.cloned.1.call-start
  8.0 0.7 fusion.5
  8.7 0.1 copy-done
  8.8 0.6 gather_fusion
  9.4 2.7 %select_convert_fusion = bf16[8,128,512]{2,1,0:T(8,128)(2,1)} fusion(bf16[8,128,128]{2,1,0:T(8,128)(2,1)S(1)} %gather_fusion, bf16[8,128,512]{2,1,0:T(8,128)(2,1)} %bitcast.25, pred[8]{0:T(512)(128)(4,1)S(1)} %iota_compare_fusion.2), kind=kOutput, calls=%fused_computation.3 | convolution fusion | flops 135266304 | bytes 2359304 | tf_op jit(solution)/shard_map/isab,isbm->isam/dot_general | solution.py:14
  12.1 0.0 all-gather.2.cloned.1.call-update
  12.1 0.0 reduce-scatter.2.cloned.1.call-start
  12.1 83.6 %all-gather.2.cloned.1.call-done = bf16[1,1024,2048]{2,1,0:T(8,128)(2,1)} async-done(((bf16[1,1024,512]{2,1,0:T(8,128)(2,1)}), bf16[1,1024,2048]{2,1,0:T(8,128)(2,1)}) %all-gather.2.cloned.1.call-update) | async-done | bytes 4194320 | tf_op jit(solution)/shard_map/all_gather | solution.py:30
  95.7 6.8 %fusion = f32[512,2048]{1,0:T(8,128)} fusion(bf16[1024,512]{1,0:T(8,128)(2,1)} %bitcast.24, bf16[1,1024,2048]{2,1,0:T(8,128)(2,1)} %all-gather.2.cloned.1.call-done), kind=kOutput, calls=%fused_computation.1 | convolution fusion | flops 2147483648 | bytes 9437184 | tf_op jit(solution)/shard_map/ipm,ipn->mn/dot_general | solution.py:27
  102.5 0.0 copy-start.1
  102.5 0.0 copy-start.2
  102.5 0.0 copy-start.3
  102.5 0.0 reduce-scatter.2.cloned.1.call-update
  102.6 1.2 copy-done.1
  103.8 0.0 copy-done.2
  103.8 0.4 fusion.2
  104.1 0.0 copy-done.3
  104.1 0.3 convolution_bitcast_fusion
  104.4 39.3 %psum.7 = f32[8192]{0:T(1024)} all-reduce(f32[8192]{0:T(1024)S(1)} %convolution_bitcast_fusion), channel_id=1, replica_groups=mesh['occ'=8,'ao'=4] {'occ','ao'}, use_global_device_ids=true, to_apply=%region_1.2 | all-reduce | flops 8192 | bytes 65536 | tf_op jit(solution)/shard_map/psum | solution.py:25
  143.7 8.8 %reduce-scatter.2.cloned.1.call-done = f32[512,256]{1,0:T(8,128)} async-done(((f32[512,2048]{1,0:T(8,128)}), f32[512,256]{1,0:T(8,128)}) %reduce-scatter.2.cloned.1.call-update) | async-done | bytes 524304 | tf_op jit(solution)/shard_map/reduce_scatter | solution.py:33
  (2 shorter events, 0.0 us)
Async XLA Ops:
  7.2 1.6 %copy-start = (bf16[64,128,128]{2,1,0:T(8,128)(2,1)S(1)}, bf16[64,128,128]{2,1,0:T(8,128)(2,1)}, u32[]{:S(2)}) copy-start(bf16[64,128,128]{2,1,0:T(8,128)(2,1)} %param.7) | copy-start | bytes 6291460
  7.2 88.5 %all-gather.2.cloned.1.call-start = ((), (), s32[]{:S(2)}) async-start(), calls=%async_computation.1 | async-start | bytes 5242880 | tf_op jit(solution)/shard_map/all_gather | solution.py:30
  12.1 140.4 %reduce-scatter.2.cloned.1.call-start = ((), (), s32[]{:S(2)}) async-start(), calls=%async_computation.2 | async-start | bytes 4718592 | tf_op jit(solution)/shard_map/reduce_scatter | solution.py:33
  102.5 1.2 copy-start.1
  102.5 1.2 copy-start.2
  102.5 1.6 copy-start.3
Sparse Core Ops, SparseCore 0:
  12.2 83.4 all-gather.1
  102.7 49.7 reduce-scatter.1
where the time goes:
time: 160 us; the launch traced here: 159 us
  waiting for transfers between devices  92.3 us (58%)
  blocking collectives  39.3 us (25%)
  between operations  14.8 us (9%)
  matrix products  10.2 us (6%)
  local copies, waits for them, and re-layouts  1.89 us (1%)
    all_gather x1, waiting for transfers between devices, on_device(): lax.all_gather(fitted, 'ao', axis=2, tiled=True)  83.6 us
    psum x1, blocking collectives, on_device(): density = lax.psum(local_density, ('occ', 'ao'))  39.3 us
    reduce_scatter x1, waiting for transfers between devices, on_device(): lax.psum_scatter(partial_value, 'occ', scatter_dimension=1, tiled=True)  8.75 us
    dot_general x1, matrix products, on_device(): jnp.einsum('ipm,ipn->mn', fitted, lax.all_gather(fitted, 'ao', axis=2, ti...  6.82 us
  transfers between devices with their start and end apart: 2, of which 2 were waited for; matrix products, arithmetic and copies ran while one was open for 0% of the time, Pallas kernels for 0%

commit v1 on v0

--- a/solution.py
+++ b/solution.py
@@ -24,12 +24,23 @@
     local_density = jnp.einsum("isf,isr->fr", one_hot, pair_part.reshape(lmo_count, slots, block))
     density = lax.psum(local_density, ("occ", "ao"))
     density = density.reshape(fit_blocks * block)
-    partial_value = jnp.einsum(
-        "ipm,ipn->mn",
-        fitted,
-        lax.all_gather(fitted, "ao", axis=2, tiled=True),
-        preferred_element_type=jnp.float32,
-    )
+    d_next = lax.axis_size("ao")
+    main, s_next, f_now = (d_next, lax.axis_index("ao"), fitted.shape[2])
+    fields = [(j0, (j0 + 1) % main) for j0 in range(main)]
+    shaped, partial_value = (fitted, None)
+    for ix in range(main):
+        response = (s_next - ix) % main
+        t1 = lax.ppermute(shaped, "ao", perm=fields) if ix < main - 1 else None
+        finding = jnp.einsum("ipm,ipn->mn", fitted, shaped, preferred_element_type=jnp.float32)
+        front = finding.shape[1]
+        if partial_value is None:
+            partial_value = jnp.zeros(
+                (*finding.shape[:1], main * front, *finding.shape[2:]), finding.dtype
+            )
+        partial_value = lax.dynamic_update_slice_in_dim(
+            partial_value, finding, response * front, axis=1
+        )
+        shaped = t1
     exchange_k = lax.psum_scatter(partial_value, "occ", scatter_dimension=1, tiled=True)
     return (exchange_k, density)
 

time: 160 us -> 152 us (0.950)
  waiting for transfers between devices: 92.3 us -> 78.2 us
  starting transfers between devices: 0.08 us -> 3.14 us
  local copies, waits for them, and re-layouts: 1.89 us -> 4.13 us
  matrix products: 10.2 us -> 11.9 us
    all_gather x1 -> x0, waiting for transfers between devices: 83.6 us -> none  [on_device(): lax.all_gather(fitted, 'ao', axis=2, tiled=True)]
    ppermute x0 -> x3, waiting for transfers between devices: none -> 67.9 us  [on_device(): t1 = lax.ppermute(shaped, 'ao', perm=fields) if ix < main - 1 else None]
    ppermute x0 -> x3, starting transfers between devices: none -> 3.11 us  [on_device(): t1 = lax.ppermute(shaped, 'ao', perm=fields) if ix < main - 1 else None]
    dot_general x1 -> x4, matrix products: 6.82 us -> 9.56 us  [on_device(): jnp.einsum('ipm,ipn->mn', fitted, shaped, preferred_element_type=jnp.floa...]
    broadcast_in_dim x0 -> x1, local copies, waits for them, and re-layouts: none -> 2.45 us  [on_device(): jnp.zeros((*finding.shape[:1], main * front, *finding.shape[2:]), finding...]
  transfers between devices with their start and end apart: 2 -> 4, of which waited for: 2 -> 4; matrix products, arithmetic and copies ran while one was open for 0% -> 6% of each run, Pallas kernels for 0% -> 0%
where the time goes in v1:
time: 152 us; the launch traced here: 151 us
  waiting for transfers between devices  78.2 us (51%)
  blocking collectives  38.3 us (25%)
  between operations  14.7 us (10%)
  matrix products  11.9 us (8%)
  local copies, waits for them, and re-layouts  4.13 us (3%)
  starting transfers between devices  3.14 us (2%)
    ppermute x3, waiting for transfers between devices, on_device(): t1 = lax.ppermute(shaped, 'ao', perm=fields) if ix < main - 1 else None  67.9 us
    psum x1, blocking collectives, on_device(): density = lax.psum(local_density, ('occ', 'ao'))  38.3 us
    reduce_scatter x1, waiting for transfers between devices, on_device(): lax.psum_scatter(partial_value, 'occ', scatter_dimension=1, tiled=True)  10.3 us
    dot_general x4, matrix products, on_device(): jnp.einsum('ipm,ipn->mn', fitted, shaped, preferred_element_type=jnp.floa...  9.56 us
    ppermute x3, starting transfers between devices, on_device(): t1 = lax.ppermute(shaped, 'ao', perm=fields) if ix < main - 1 else None  3.11 us
  transfers between devices with their start and end apart: 4, of which 4 were waited for; matrix products, arithmetic and copies ran while one was open for 6% of the time, Pallas kernels for 0%

profile of v1, /device:TPU:0, one launch (start us, length us, event | category | flops | bytes accessed | tf_op | source)
XLA Modules:
  0.0 151.2 jit_solution(614908930677177998)
XLA Ops:
  7.2 0.0 copy-start
  7.2 0.0 reduce-scatter.2.cloned.1.call-start
  7.2 0.8 fusion.7
  8.7 0.1 copy-done
  8.8 0.6 gather_fusion
  9.4 1.6 %select_convert_fusion = bf16[8,128,512]{2,1,0:T(8,128)(2,1)S(1)} fusion(bf16[8,128,128]{2,1,0:T(8,128)(2,1)S(1)} %gather_fusion, bf16[8,128,512]{2,1,0:T(8,128)(2,1)} %bitcast.41, pred[8]{0:T(512)(128)(4,1)S(1)} %iota_compare_fusion.2), kind=kOutput, calls=%fused_computation.1 | convolution fusion | flops 135266304 | bytes 2359304 | tf_op jit(solution)/shard_map/isab,isbm->isam/dot_general | solution.py:14
  11.0 3.1 %collective-permute-start = (bf16[1,1024,512]{2,1,0:T(8,128)(2,1)S(1)}, bf16[1,1024,512]{2,1,0:T(8,128)(2,1)S(1)}, u32[]{:S(2)}, u32[]{:S(2)}) collective-permute-start(bf16[1,1024,512]{2,1,0:T(8,128)(2,1)S(1)} %bitcast.37), channel_id=1, source_target_pairs={{0,1},{1,2},{2,3},{3,0},{4,5},{5,6},{6,7},{7,4},{8,9},{9,10},{10,1... | collective-permute-start | bytes 3145736 | tf_op jit(solution)/shard_map/ppermute | solution.py:33
  14.1 25.2 %collective-permute-done = bf16[1,1024,512]{2,1,0:T(8,128)(2,1)S(1)} collective-permute-done((bf16[1,1024,512]{2,1,0:T(8,128)(2,1)S(1)}, bf16[1,1024,512]{2,1,0:T(8,128)(2,1)S(1)}, u32[]{:S(2)}, u32[]{:S(2)}) %collective-permute-start) | collective-permute-done | bytes 1048608 | tf_op jit(solution)/shard_map/ppermute | solution.py:33
  39.3 0.0 copy-start.2
  39.3 1.0 copy-done.2
  40.3 0.0 collective-permute-start.1
  40.3 26.2 %collective-permute-done.1 = bf16[1,1024,512]{2,1,0:T(8,128)(2,1)} collective-permute-done((bf16[1,1024,512]{2,1,0:T(8,128)(2,1)S(1)}, bf16[1,1024,512]{2,1,0:T(8,128)(2,1)}, u32[]{:S(2)}, u32[]{:S(2)}) %collective-permute-start.1) | collective-permute-done | bytes 1048608 | tf_op jit(solution)/shard_map/ppermute | solution.py:33
  66.5 0.0 collective-permute-start.2
  66.5 0.0 copy-start.3
  66.5 2.4 %broadcast_in_dim.23 = f32[512,2048]{1,0:T(8,128)} broadcast(f32[]{:T(128)} %constant.38.clone.1), dimensions={} | broadcast | bytes 4194308 | tf_op jit(solution)/shard_map/broadcast_in_dim | solution.py:37
  69.0 1.8 %fusion = f32[512,2048]{1,0:T(8,128)} fusion(f32[512,2048]{1,0:T(8,128)} %broadcast_in_dim.23, s32[]{:T(128)S(6)} %select_n.42, bf16[8,128,512]{2,1,0:T(8,128)(2,1)S(1)} %select_convert_fusion), kind=kOutput, calls=%fused_computation.6 | convolution fusion | flops 536870912 | bytes 3145732 | tf_op jit(solution)/shard_map/ipm,ipn->mn/dot_general | solution.py:34
  70.7 0.0 copy-done.3
  70.7 1.8 %convolution_dynamic-update-slice_fusion.2 = f32[512,2048]{1,0:T(8,128)} fusion(f32[512,2048]{1,0:T(8,128)} %fusion, s32[]{:T(128)S(6)} %select_n.44, bf16[1024,512]{1,0:T(8,128)(2,1)S(1)} %bitcast.38, bf16[1,1024,512]{2,1,0:T(8,128)(2,1)S(1)} %copy-done.3), kind=kOutput, calls=%fused_computation.4 | convolution fusion | flops 536870912 | bytes 3145732 | tf_op jit(solution)/shard_map/ipm,ipn->mn/dot_general | solution.py:34
  72.6 3.0 %convolution_dynamic-update-slice_fusion.1 = f32[512,2048]{1,0:T(8,128)} fusion(f32[512,2048]{1,0:T(8,128)} %convolution_dynamic-update-slice_fusion.2, s32[]{:T(128)S(6)} %select_n.46, bf16[1024,512]{1,0:T(8,128)(2,1)S(1)} %bitcast.39, bf16[1,1024,512]{2,1,0:T(8,128)(2,1)} %collective-permute-done.1), kind=kOutput, calls=%fused_computation.3 | convolution fusion | flops 536870912 | bytes 3145732 | tf_op jit(solution)/shard_map/ipm,ipn->mn/dot_general | solution.py:34
  75.6 0.0 copy-start.1
  75.6 0.0 copy-start.4
  75.6 16.5 %collective-permute-done.2 = bf16[1,1024,512]{2,1,0:T(8,128)(2,1)} collective-permute-done((bf16[1,1024,512]{2,1,0:T(8,128)(2,1)}, bf16[1,1024,512]{2,1,0:T(8,128)(2,1)}, u32[]{:S(2)}, u32[]{:S(2)}) %collective-permute-start.2) | collective-permute-done | bytes 1048608 | tf_op jit(solution)/shard_map/ppermute | solution.py:33
  92.1 3.0 %convolution_dynamic-update-slice_fusion = f32[512,2048]{1,0:T(8,128)} fusion(f32[512,2048]{1,0:T(8,128)} %convolution_dynamic-update-slice_fusion.1, s32[]{:T(128)S(6)} %select_n.48, bf16[1024,512]{1,0:T(8,128)(2,1)S(1)} %bitcast.40, bf16[1,1024,512]{2,1,0:T(8,128)(2,1)} %collective-permute-done.2), kind=kOutput, calls=%fused_computation.2 | convolution fusion | flops 536870912 | bytes 3145732 | tf_op jit(solution)/shard_map/ipm,ipn->mn/dot_general | solution.py:34
  95.1 0.0 reduce-scatter.2.cloned.1.call-update
  95.1 0.0 copy-done.1
  95.1 0.4 fusion.4
  95.5 0.0 copy-done.4
  95.5 0.3 convolution_bitcast_fusion.1
  95.7 38.3 %psum.7 = f32[8192]{0:T(1024)} all-reduce(f32[8192]{0:T(1024)S(1)} %convolution_bitcast_fusion.1), channel_id=1, replica_groups=mesh['occ'=8,'ao'=4] {'occ','ao'}, use_global_device_ids=true, to_apply=%region_1.2 | all-reduce | flops 8192 | bytes 65536 | tf_op jit(solution)/shard_map/psum | solution.py:25
  134.1 10.3 %reduce-scatter.2.cloned.1.call-done = f32[512,256]{1,0:T(8,128)} async-done(((f32[512,2048]{1,0:T(8,128)}), f32[512,256]{1,0:T(8,128)}) %reduce-scatter.2.cloned.1.call-update) | async-done | bytes 524304 | tf_op jit(solution)/shard_map/reduce_scatter | solution.py:44
  (2 shorter events, 0.0 us)
Async XLA Ops:
  7.2 1.6 %copy-start = (bf16[64,128,128]{2,1,0:T(8,128)(2,1)S(1)}, bf16[64,128,128]{2,1,0:T(8,128)(2,1)}, u32[]{:S(2)}) copy-start(bf16[64,128,128]{2,1,0:T(8,128)(2,1)} %param.7) | copy-start | bytes 6291460
  7.2 137.2 %reduce-scatter.2.cloned.1.call-start = ((), (), s32[]{:S(2)}) async-start(), calls=%async_computation.1 | async-start | bytes 4718592 | tf_op jit(solution)/shard_map/reduce_scatter | solution.py:44
  11.0 28.3 %collective-permute-start = (bf16[1,1024,512]{2,1,0:T(8,128)(2,1)S(1)}, bf16[1,1024,512]{2,1,0:T(8,128)(2,1)S(1)}, u32[]{:S(2)}, u32[]{:S(2)}) collective-permute-start(bf16[1,1024,512]{2,1,0:T(8,128)(2,1)S(1)} %bitcast.37), channel_id=1, source_target_pairs={{0,1},{1,2},{2,3},{3,0},{4,5},{5,6},{6,7},{7,4},{8,9},{9,10},{10,1... | collective-permute-start | bytes 3145736 | tf_op jit(solution)/shard_map/ppermute | solution.py:33
  39.3 1.0 copy-start.2
  40.3 26.2 %collective-permute-start.1 = (bf16[1,1024,512]{2,1,0:T(8,128)(2,1)S(1)}, bf16[1,1024,512]{2,1,0:T(8,128)(2,1)}, u32[]{:S(2)}, u32[]{:S(2)}) collective-permute-start(bf16[1,1024,512]{2,1,0:T(8,128)(2,1)S(1)} %collective-permute-done), channel_id=1, source_target_pairs={{0,1},{1,2},{2,3},{3,0},{4,5},{5,6},{6,7},{7,4},{8,9},{9,10},{10,1... | collective-permute-start | bytes 3145736 | tf_op jit(solution)/shard_map/ppermute | solution.py:33
  66.5 25.6 %collective-permute-start.2 = (bf16[1,1024,512]{2,1,0:T(8,128)(2,1)}, bf16[1,1024,512]{2,1,0:T(8,128)(2,1)}, u32[]{:S(2)}, u32[]{:S(2)}) collective-permute-start(bf16[1,1024,512]{2,1,0:T(8,128)(2,1)} %collective-permute-done.1), channel_id=1, source_target_pairs={{0,1},{1,2},{2,3},{3,0},{4,5},{5,6},{6,7},{7,4},{8,9},{9,10},{10,1... | collective-permute-start | bytes 3145736 | tf_op jit(solution)/shard_map/ppermute | solution.py:33
  66.5 4.2 %copy-start.3 = (bf16[1,1024,512]{2,1,0:T(8,128)(2,1)S(1)}, bf16[1,1024,512]{2,1,0:T(8,128)(2,1)}, u32[]{:S(2)}) copy-start(bf16[1,1024,512]{2,1,0:T(8,128)(2,1)} %copy-done.2) | copy-start | bytes 3145732
  75.6 19.5 %copy-start.1 = (bf16[512,1]{0,1:T(2,128)(2,1)S(1)}, bf16[512,1]{0,1:T(2,128)(2,1)}, u32[]{:S(2)}) copy-start(bf16[512,1]{0,1:T(2,128)(2,1)} %param.5) | copy-start | bytes 3076
  75.6 19.9 %copy-start.4 = (s32[1,8]{1,0:T(1,128)S(1)}, s32[1,8]{1,0:T(1,128)}, u32[]{:S(2)}) copy-start(s32[1,8]{1,0:T(1,128)} %param.8) | copy-start | bytes 100
Sparse Core Ops, SparseCore 0:
  95.2 49.0 reduce-scatter.1
